TPU v7x, 256 devices: a whole 4x4x8 slice. The times are simulated.
256 devices in a mesh: dp: 16 (over z, core), vocab: 16 (over x, y).
Axes of the slice: x: 4, y: 4, z: 8, core: 2. Of those that a mesh axis runs over, the one named last changes fastest.
Arguments:
- hidden: bfloat16 [4096, 4096], P('dp')
- table: bfloat16 [16384, 4096], P(('vocab', 'dp')), as said below
- targets: int32 [4096], P('dp'), may hold values from 0 to 16383
- token_scale: float32 [4096], P('dp'), may hold values from 2 to 32
- enc_ids: int32 [4096], P(('dp', 'vocab')), may hold values from 0 to 16383
- enc_cot: bfloat16 [4096, 4096], P(('dp', 'vocab')), may hold values from -6 to 6
- dec_ids: int32 [4096], P(('dp', 'vocab')), may hold values from 0 to 16383
- dec_cot: bfloat16 [4096, 4096], P(('dp', 'vocab')), may hold values from -6 to 6
Outputs:
- grad_hidden: bfloat16 [4096, 4096], P('dp', 'vocab')
- grad_table: float32 [16384, 4096], P(('vocab', 'dp'))
- loss: float32 [4096], P('dp')
Inputs may be any that keep to these rules, and one draw needn't show every extreme that they name: table entries of order 3 / sqrt(4096).
All inputs are finite; a program needn't handle non-finite values.
Results may differ from a plain program's by a relative error of at most 0.018.
Values may be sent and summed in bfloat16 or wider, within the bound.
No kernel may reach another device: no remote copies, remote signals or barrier semaphores. Data moves between devices by JAX's collectives and lax.ppermute only.
A program may use at most 128 MiB of HBM per device.

v0:
```python
import jax
import jax.numpy as jnp
from jax import lax
from jax.sharding import PartitionSpec as P


def shards(hidden, table, targets, token_scale, enc_ids, enc_cot, dec_ids, dec_cot):
    vocab_rows = table.shape[0] * lax.axis_size("dp")
    offset = lax.axis_index("vocab") * vocab_rows
    gathered = lax.all_gather(table, "dp", axis=0, tiled=True)
    logits = jnp.dot(hidden, gathered.T, preferred_element_type=jnp.float32)
    local_target = targets - offset
    columns = jnp.arange(vocab_rows, dtype=jnp.int32)
    matches = columns[None, :] == local_target[:, None]
    target_part = jnp.sum(jnp.where(matches, logits, 0.0), axis=1)
    local_max = jnp.max(logits, axis=1)
    row_max = lax.pmax(local_max, "vocab")
    expo = jnp.exp(logits - row_max[:, None])
    row_sum, target_logit = lax.psum((jnp.sum(expo, axis=1), target_part), "vocab")
    loss = row_max + jnp.log(row_sum) - target_logit
    dlogits = (
        token_scale[:, None] * (expo / row_sum[:, None] - matches.astype(jnp.float32))
    ).astype(jnp.bfloat16)
    state_term = jnp.dot(dlogits, gathered, preferred_element_type=jnp.float32)
    grad_hidden = lax.psum_scatter(
        state_term.astype(jnp.bfloat16), "vocab", scatter_dimension=1, tiled=True
    )
    ids_one, cot_one, ids_two, cot_two = (
        lax.all_gather(enc_ids, "vocab", axis=0, tiled=True),
        lax.all_gather(enc_cot, "vocab", axis=0, tiled=True),
        lax.all_gather(dec_ids, "vocab", axis=0, tiled=True),
        lax.all_gather(dec_cot, "vocab", axis=0, tiled=True),
    )
    all_ids = jnp.concatenate([ids_one, ids_two], axis=0) - offset
    all_cot = jnp.concatenate([cot_one, cot_two], axis=0)
    hits = (columns[:, None] == all_ids[None, :]).astype(jnp.bfloat16)
    looked_up = jnp.dot(hits, all_cot, preferred_element_type=jnp.float32)
    head = lax.dot_general(
        dlogits, hidden, (((0,), (0,)), ((), ())), preferred_element_type=jnp.float32
    )
    grad_table = lax.psum_scatter(
        (head + looked_up).astype(jnp.bfloat16), "dp", scatter_dimension=0, tiled=True
    ).astype(jnp.float32)
    return (grad_hidden, grad_table, loss)


def solution(mesh):
    placed = (
        P("dp", None),
        P(("vocab", "dp"), None),
        P("dp"),
        P("dp"),
        P(("dp", "vocab")),
        P(("dp", "vocab"), None),
        P(("dp", "vocab")),
        P(("dp", "vocab"), None),
    )
    return jax.shard_map(
        shards,
        mesh=mesh,
        in_specs=placed,
        out_specs=(P("dp", "vocab"), P(("vocab", "dp"), None), P("dp")),
        check_vma=False,
    )
```

profile of v0, /device:TPU:32, one launch (start us, length us, event | category | flops | bytes accessed | tf_op | source)
XLA Modules:
  0.0 417.9 jit_solution(18154777926044538096)
XLA Ops:
  7.2 0.7 all-gather.6.cloned.1.call-update
  8.0 0.7 all-gather.8.cloned.1.call-update
  8.7 0.7 all-gather.4.cloned.1.call-update
  9.4 0.0 reduce-scatter.5.cloned.1.call-start
  9.4 1.3 dynamic-slice
  11.4 0.9 dynamic-update-slice.1
  12.2 0.8 dynamic-update-slice
  13.1 16.5 %all-reduce.2 = (s32[256]{0:T(256)S(1)}, s32[256]{0:T(256)S(1)}) all-reduce(s32[256]{0:T(256)S(1)} %dynamic-update-slice.1, s32[256]{0:T(256)S(1)} %dynamic-update-slice), channel_id=1, replica_groups=mesh['dp'=16,'vocab'=16] {'vocab'}, use_global_device_ids=true, to_apply=%add.1 | all-reduce | flops 512 | bytes 4096
  29.5 0.7 broadcast_subtract_fusion
  30.2 32.8 %all-gather.6.cloned.1.call-done = bf16[256,4096]{1,0:T(8,128)(2,1)} async-done(((bf16[16,4096]{1,0:T(8,128)(2,1)}), bf16[256,4096]{1,0:T(8,128)(2,1)}) %all-gather.6.cloned.1.call-update) | async-done | bytes 2097168 | tf_op jit(solution)/shard_map/all_gather | solution.py:30
  63.0 51.8 %all-gather.8.cloned.1.call-done = bf16[256,4096]{1,0:T(8,128)(2,1)} async-done(((bf16[16,4096]{1,0:T(8,128)(2,1)}), bf16[256,4096]{1,0:T(8,128)(2,1)}) %all-gather.8.cloned.1.call-update) | async-done | bytes 2097168 | tf_op jit(solution)/shard_map/all_gather | solution.py:32
  114.8 10.3 %fusion = f32[1024,4096]{1,0:T(8,128)} fusion(bf16[256,4096]{1,0:T(8,128)(2,1)} %all-gather.8.cloned.1.call-done, bf16[256,4096]{1,0:T(8,128)(2,1)} %all-gather.6.cloned.1.call-done, s32[512]{0:T(512)S(1)} %add_subtract_fusion), kind=kOutput, calls=%fused_computation.2 | convolution fusion | flops 4303880192 | bytes 20973568 | tf_op jit(solution)/shard_map/dot_general | solution.py:37
  125.1 45.1 %all-gather.4.cloned.1.call-done = bf16[1024,4096]{1,0:T(8,128)(2,1)} async-done(((bf16[64,4096]{1,0:T(8,128)(2,1)}), bf16[1024,4096]{1,0:T(8,128)(2,1)}) %all-gather.4.cloned.1.call-update) | async-done | bytes 8388624 | tf_op jit(solution)/shard_map/all_gather | solution.py:10
  170.2 5.8 %fusion.7 = (f32[256]{0:T(256)S(1)}, f32[256,1024]{1,0:T(8,128)S(1)}) fusion(bf16[256,4096]{1,0:T(8,128)(2,1)S(1)} %copy-done, bf16[1024,4096]{1,0:T(8,128)(2,1)} %all-gather.4.cloned.1.call-done), kind=kOutput, calls=%fused_computation.17 | convolution fusion | flops 2147745536 | bytes 11535360 | tf_op jit(solution)/shard_map/dot_general | solution.py:11
  176.0 40.3 %pmax.7 = f32[256]{0:T(256)S(1)} all-reduce(f32[256]{0:T(256)S(1)} %get-tuple-element.9), channel_id=1, replica_groups=mesh['dp'=16,'vocab'=16] {'vocab'}, use_global_device_ids=true, to_apply=%region_1.2 | all-reduce | flops 256 | bytes 2048 | tf_op jit(solution)/shard_map/pmax | solution.py:17
  216.4 0.5 select_reduce_fusion
  216.8 35.5 %all-reduce.3 = (f32[256]{0:T(256)S(1)}, f32[256]{0:T(256)S(1)}) all-reduce(f32[256]{0:T(256)S(1)} %get-tuple-element.4, f32[256]{0:T(256)S(1)} %get-tuple-element.3), channel_id=1, replica_groups=mesh['dp'=16,'vocab'=16] {'vocab'}, use_global_device_ids=true, to_apply=%region_3.4 | all-reduce | flops 512 | bytes 4096 | tf_op jit(solution)/shard_map/psum | solution.py:19
  252.3 9.2 %add_convert_fusion = bf16[1024,4096]{1,0:T(8,128)(2,1)} fusion(f32[1024,4096]{1,0:T(8,128)} %fusion, bf16[256,4096]{1,0:T(8,128)(2,1)S(1)} %copy-done, f32[256,1024]{1,0:T(8,128)S(1)} %get-tuple-element.10, s32[256]{0:T(256)S(1)} %broadcast_subtract_fusion, f32[256]{0:T(256)S(1)} %get-tuple-element.7, f32[256]{0:T(256)S(1)} %pmax.7, f32[256]{0:T(256)S(1)} %copy-done.1), kind=kOutput, calls=%fused_computation | convolution fusion | flops 2157707264 | bytes 28315648 | tf_op jit(solution)/shard_map/dot_general | solution.py:38
  261.5 0.0 reduce-scatter.3.cloned.1.call-start
  261.6 7.4 %convolution_convert_fusion = bf16[256,4096]{1,0:T(8,128)(2,1)} fusion(bf16[1024,4096]{1,0:T(8,128)(2,1)} %all-gather.4.cloned.1.call-done, f32[256,1024]{1,0:T(8,128)S(1)} %get-tuple-element.10, s32[256]{0:T(256)S(1)} %broadcast_subtract_fusion, f32[256]{0:T(256)S(1)} %get-tuple-element.7, f32[256]{0:T(256)S(1)} %pmax.7, f32[256]{0:T(256)S(1)} %copy-done.1), kind=kOutput, calls=%fused_computation.1 | convolution fusion | flops 2150367232 | bytes 11538432 | tf_op jit(solution)/shard_map/dot_general | solution.py:24
  269.0 0.6 add_subtract_fusion.1
  269.5 56.1 %reduce-scatter.5.cloned.1.call-done = bf16[64,4096]{1,0:T(8,128)(2,1)} async-done(((bf16[1024,4096]{1,0:T(8,128)(2,1)}), bf16[64,4096]{1,0:T(8,128)(2,1)}) %reduce-scatter.5.cloned.1.call-update) | async-done | bytes 524304 | tf_op jit(solution)/shard_map/reduce_scatter | solution.py:41
  325.6 2.1 convert_element_type.20
  327.7 83.7 %reduce-scatter.3.cloned.1.call-done = bf16[256,256]{1,0:T(8,128)(2,1)} async-done(((bf16[256,4096]{1,0:T(8,128)(2,1)}), bf16[256,256]{1,0:T(8,128)(2,1)}) %reduce-scatter.3.cloned.1.call-update) | async-done | bytes 131088 | tf_op jit(solution)/shard_map/reduce_scatter | solution.py:25
  (12 shorter events, 0.2 us)
Async XLA Ops:
  7.2 163.1 %copy-start = (bf16[256,4096]{1,0:T(8,128)(2,1)S(1)}, bf16[256,4096]{1,0:T(8,128)(2,1)}, u32[]{:S(2)}) copy-start(bf16[256,4096]{1,0:T(8,128)(2,1)} %param.8) | copy-start | bytes 6291460
  7.2 55.8 %all-gather.6.cloned.1.call-start = ((), (), s32[]{:S(2)}) async-start(), calls=%async_computation.4 | async-start | bytes 2228224 | tf_op jit(solution)/shard_map/all_gather | solution.py:30
  7.9 106.9 %all-gather.8.cloned.1.call-start = ((), (), s32[]{:S(2)}) async-start(), calls=%async_computation.5 | async-start | bytes 2228224 | tf_op jit(solution)/shard_map/all_gather | solution.py:32
  8.7 161.5 %all-gather.4.cloned.1.call-start = ((), (), s32[]{:S(2)}) async-start(), calls=%async_computation.2 | async-start | bytes 8912896 | tf_op jit(solution)/shard_map/all_gather | solution.py:10
  9.4 316.2 %reduce-scatter.5.cloned.1.call-start = ((), (), s32[]{:S(2)}) async-start(), calls=%async_computation.6 | async-start | bytes 8912896 | tf_op jit(solution)/shard_map/reduce_scatter | solution.py:41
  125.1 127.2 %copy-start.1 = (f32[256]{0:T(256)S(1)}, f32[256]{0:T(256)}, u32[]{:S(2)}) copy-start(f32[256]{0:T(256)} %param.11) | copy-start | bytes 3076
  261.5 149.9 %reduce-scatter.3.cloned.1.call-start = ((), (), s32[]{:S(2)}) async-start(), calls=%async_computation.3 | async-start | bytes 2228224 | tf_op jit(solution)/shard_map/reduce_scatter | solution.py:25
Sparse Core Ops, SparseCore 0:
  10.4 52.5 all-gather.5
  65.5 49.3 all-gather.7
  116.7 53.4 all-gather.3
  261.6 63.9 reduce-scatter.4
  329.6 81.7 reduce-scatter.2
where the time goes:
time: 418 us
  waiting for transfers between devices  272 us (65%)
  blocking collectives  92.2 us (22%)
  matrix products  32.7 us (8%)
  between operations  14.5 us (3%)
    reduce_scatter x1, waiting for transfers between devices, shards(): lax.psum_scatter(state_term.astype(jnp.bfloat16), 'vocab', scatter_dimens...  83.7 us
    reduce_scatter x1, waiting for transfers between devices, shards(): lax.psum_scatter((head + looked_up).astype(jnp.bfloat16), 'dp', scatter_d...  56.1 us
    all_gather x1, waiting for transfers between devices, shards(): lax.all_gather(dec_cot, 'vocab', axis=0, tiled=True)  51.8 us
    all_gather x1, waiting for transfers between devices, shards(): gathered = lax.all_gather(table, 'dp', axis=0, tiled=True)  45.1 us
    pmax x1, blocking collectives, shards(): row_max = lax.pmax(local_max, 'vocab')  40.3 us
    psum x1, blocking collectives, shards(): lax.psum((jnp.sum(expo, axis=1), target_part), 'vocab')  35.5 us
    all_gather x1, waiting for transfers between devices, shards(): lax.all_gather(enc_cot, 'vocab', axis=0, tiled=True)  32.8 us
    unnamed x1, blocking collectives  16.5 us
  transfers between devices with their start and end apart: 5, of which 5 were waited for; matrix products, arithmetic and copies ran while one was open for 6% of the time, Pallas kernels for 0%

commit v1 on v0

--- a/solution.py
+++ b/solution.py
@@ -7,7 +7,24 @@
 def shards(hidden, table, targets, token_scale, enc_ids, enc_cot, dec_ids, dec_cot):
     vocab_rows = table.shape[0] * lax.axis_size("dp")
     offset = lax.axis_index("vocab") * vocab_rows
-    gathered = lax.all_gather(table, "dp", axis=0, tiled=True)
+    devices, index, rows = (lax.axis_size("dp"), lax.axis_index("dp"), table.shape[0])
+    right = [(i, (i + 1) % devices) for i in range(devices)]
+    left = [(i, (i - 1) % devices) for i in range(devices)]
+    out = jnp.zeros((*table.shape[:0], devices * rows, *table.shape[0 + 1 :]), table.dtype)
+    out = lax.dynamic_update_slice_in_dim(out, table, index * rows, axis=0)
+    from_left = from_right = table
+    halfway = devices // 2
+    for step in range(1, halfway + 1):
+        from_left = lax.ppermute(from_left, "dp", right)
+        out = lax.dynamic_update_slice_in_dim(
+            out, from_left, (index - step) % devices * rows, axis=0
+        )
+        if step < devices - halfway:
+            from_right = lax.ppermute(from_right, "dp", left)
+            out = lax.dynamic_update_slice_in_dim(
+                out, from_right, (index + step) % devices * rows, axis=0
+            )
+    gathered = out
     logits = jnp.dot(hidden, gathered.T, preferred_element_type=jnp.float32)
     local_target = targets - offset
     columns = jnp.arange(vocab_rows, dtype=jnp.int32)

time: 418 us -> 375 us (0.90)
  waiting for transfers between devices: 272 us -> 195 us
  local copies, waits for them, and re-layouts: 2.98 us -> 21.8 us
  starting transfers between devices: 0.19 us -> 14.6 us
    all_gather x1, waiting for transfers between devices: 51.8 us -> 0.01 us  [shards(): lax.all_gather(dec_cot, 'vocab', axis=0, tiled=True)]
    all_gather x1 -> x0, waiting for transfers between devices: 45.1 us -> none  [shards(): gathered = lax.all_gather(table, 'dp', axis=0, tiled=True)]
    ppermute x0 -> x15, waiting for transfers between devices: none -> 28.6 us  [the longest x8 26.5 us: shards(): from_left = lax.ppermute(from_left, 'dp', right)]
    dynamic_update_slice x0 -> x16, local copies, waits for them, and re-layouts: none -> 14.6 us  [the longest x8 7.82 us: shards(): lax.dynamic_update_slice_in_dim(out, from_left, (index - step) % devices...]
    ppermute x0 -> x15, starting transfers between devices: none -> 14.3 us  [the longest x7 14.2 us: shards(): from_right = lax.ppermute(from_right, 'dp', left)]
    all_gather x1, waiting for transfers between devices: 32.8 us -> 24.8 us  [shards(): lax.all_gather(enc_cot, 'vocab', axis=0, tiled=True)]
    broadcast_in_dim x0 -> x1, local copies, waits for them, and re-layouts: none -> 4.27 us  [shards(): jnp.zeros((*table.shape[:0], devices * rows, *table.shape[0 + 1:]), table...]
  transfers between devices with their start and end apart: 5 -> 19, of which waited for: 5 -> 13; matrix products, arithmetic and copies ran while one was open for 6% -> 11% of each run, Pallas kernels for 0% -> 0%
where the time goes in v1:
time: 375 us
  waiting for transfers between devices  195 us (52%)
  blocking collectives  90 us (24%)
  matrix products  34.8 us (9%)
  local copies, waits for them, and re-layouts  21.8 us (6%)
  between operations  14.8 us (4%)
  starting transfers between devices  14.6 us (4%)
    reduce_scatter x1, waiting for transfers between devices, shards(): lax.psum_scatter(state_term.astype(jnp.bfloat16), 'vocab', scatter_dimens...  83.8 us
    reduce_scatter x1, waiting for transfers between devices, shards(): lax.psum_scatter((head + looked_up).astype(jnp.bfloat16), 'dp', scatter_d...  56.9 us
    pmax x1, blocking collectives, shards(): row_max = lax.pmax(local_max, 'vocab')  38.1 us
    psum x1, blocking collectives, shards(): lax.psum((jnp.sum(expo, axis=1), target_part), 'vocab')  35.5 us
    ppermute x8, waiting for transfers between devices, shards(): from_left = lax.ppermute(from_left, 'dp', right)  26.5 us
    all_gather x1, waiting for transfers between devices, shards(): lax.all_gather(enc_cot, 'vocab', axis=0, tiled=True)  24.8 us
    unnamed x1, blocking collectives  16.5 us
    ppermute x7, starting transfers between devices, shards(): from_right = lax.ppermute(from_right, 'dp', left)  14.2 us
  transfers between devices with their start and end apart: 19, of which 13 were waited for; matrix products, arithmetic and copies ran while one was open for 11% of the time, Pallas kernels for 0%

profile of v1, /device:TPU:32, one launch (start us, length us, event | category | flops | bytes accessed | tf_op | source)
XLA Modules:
  0.0 374.6 jit_solution(12719598059215462117)
XLA Ops:
  14.4 16.5 %all-reduce.2 = (s32[256]{0:T(256)S(1)}, s32[256]{0:T(256)S(1)}) all-reduce(s32[256]{0:T(256)S(1)} %dynamic-update-slice.1, s32[256]{0:T(256)S(1)} %dynamic-update-slice), channel_id=1, replica_groups=mesh['dp'=16,'vocab'=16] {'vocab'}, use_global_device_ids=true, to_apply=%add.1 | all-reduce | flops 512 | bytes 4096
  30.9 4.3 %broadcast_in_dim.6 = bf16[1024,4096]{1,0:T(8,128)(2,1)} broadcast(bf16[]{:T(256)} %constant.93.clone.1), dimensions={} | broadcast | bytes 8388610 | tf_op jit(solution)/shard_map/broadcast_in_dim | solution.py:13
  37.8 1.9 constant_dynamic-update-slice_fusion.14
  40.5 4.3 %collective-permute-done.2 = bf16[64,4096]{1,0:T(8,128)(2,1)S(1)} collective-permute-done((bf16[64,4096]{1,0:T(8,128)(2,1)}, bf16[64,4096]{1,0:T(8,128)(2,1)S(1)}, u32[]{:S(2)}, u32[]{:S(2)}) %collective-permute-start.2) | collective-permute-done | bytes 524320 | tf_op jit(solution)/shard_map/ppermute | solution.py:18
  44.8 1.8 collective-permute-start.5
  48.4 5.1 %collective-permute-done.4 = bf16[64,4096]{1,0:T(8,128)(2,1)S(1)} collective-permute-done((bf16[64,4096]{1,0:T(8,128)(2,1)S(1)}, bf16[64,4096]{1,0:T(8,128)(2,1)S(1)}, u32[]{:S(2)}, u32[]{:S(2)}) %collective-permute-start.4) | collective-permute-done | bytes 524320 | tf_op jit(solution)/shard_map/ppermute | solution.py:18
  53.4 2.2 collective-permute-start.7
  57.4 4.7 %collective-permute-done.6 = bf16[64,4096]{1,0:T(8,128)(2,1)S(1)} collective-permute-done((bf16[64,4096]{1,0:T(8,128)(2,1)S(1)}, bf16[64,4096]{1,0:T(8,128)(2,1)S(1)}, u32[]{:S(2)}, u32[]{:S(2)}) %collective-permute-start.6) | collective-permute-done | bytes 524320 | tf_op jit(solution)/shard_map/ppermute | solution.py:18
  62.4 2.2 collective-permute-start.9
  66.3 4.4 %collective-permute-done.8 = bf16[64,4096]{1,0:T(8,128)(2,1)S(1)} collective-permute-done((bf16[64,4096]{1,0:T(8,128)(2,1)S(1)}, bf16[64,4096]{1,0:T(8,128)(2,1)S(1)}, u32[]{:S(2)}, u32[]{:S(2)}) %collective-permute-start.8) | collective-permute-done | bytes 524320 | tf_op jit(solution)/shard_map/ppermute | solution.py:18
  71.3 2.2 collective-permute-start.11
  75.2 4.1 %collective-permute-done.10 = bf16[64,4096]{1,0:T(8,128)(2,1)S(1)} collective-permute-done((bf16[64,4096]{1,0:T(8,128)(2,1)S(1)}, bf16[64,4096]{1,0:T(8,128)(2,1)S(1)}, u32[]{:S(2)}, u32[]{:S(2)}) %collective-permute-start.10) | collective-permute-done | bytes 524320 | tf_op jit(solution)/shard_map/ppermute | solution.py:18
  80.2 2.3 collective-permute-start.13
  84.2 3.9 %collective-permute-done.12 = bf16[64,4096]{1,0:T(8,128)(2,1)S(1)} collective-permute-done((bf16[64,4096]{1,0:T(8,128)(2,1)S(1)}, bf16[64,4096]{1,0:T(8,128)(2,1)S(1)}, u32[]{:S(2)}, u32[]{:S(2)}) %collective-permute-start.12) | collective-permute-done | bytes 524320 | tf_op jit(solution)/shard_map/ppermute | solution.py:18
  90.1 24.8 %all-gather.3.cloned.1.call-done = bf16[256,4096]{1,0:T(8,128)(2,1)} async-done(((bf16[16,4096]{1,0:T(8,128)(2,1)}), bf16[256,4096]{1,0:T(8,128)(2,1)}) %all-gather.3.cloned.1.call-update) | async-done | bytes 2097168 | tf_op jit(solution)/shard_map/all_gather | solution.py:47
  114.9 10.3 %fusion = f32[1024,4096]{1,0:T(8,128)} fusion(bf16[256,4096]{1,0:T(8,128)(2,1)} %all-gather.5.cloned.1.call-done, bf16[256,4096]{1,0:T(8,128)(2,1)} %all-gather.3.cloned.1.call-done, s32[512]{0:T(512)S(1)} %add_subtract_fusion), kind=kOutput, calls=%fused_computation.2 | convolution fusion | flops 4303880192 | bytes 20973568 | tf_op jit(solution)/shard_map/dot_general | solution.py:54
  126.0 5.8 %fusion.9 = (f32[256]{0:T(256)S(1)}, f32[1024,256]{1,0:T(8,128)S(1)}) fusion(bf16[1024,4096]{1,0:T(8,128)(2,1)} %constant_dynamic-update-slice_fusion, bf16[256,4096]{1,0:T(8,128)(2,1)S(1)} %copy-done), kind=kOutput, calls=%fused_computation.35 | convolution fusion | flops 2147745536 | bytes 11535360 | tf_op jit(solution)/shard_map/dot_general | solution.py:28
  131.8 38.1 %pmax.7 = f32[256]{0:T(256)S(1)} all-reduce(f32[256]{0:T(256)S(1)} %get-tuple-element.9), channel_id=1, replica_groups=mesh['dp'=16,'vocab'=16] {'vocab'}, use_global_device_ids=true, to_apply=%region_1.2 | all-reduce | flops 256 | bytes 2048 | tf_op jit(solution)/shard_map/pmax | solution.py:34
  170.2 35.5 %all-reduce.3 = (f32[256]{0:T(256)S(1)}, f32[256]{0:T(256)S(1)}) all-reduce(f32[256]{0:T(256)S(1)} %get-tuple-element.4, f32[256]{0:T(256)S(1)} %get-tuple-element.3), channel_id=1, replica_groups=mesh['dp'=16,'vocab'=16] {'vocab'}, use_global_device_ids=true, to_apply=%region_3.4 | all-reduce | flops 512 | bytes 4096 | tf_op jit(solution)/shard_map/psum | solution.py:36
  205.7 11.5 %add_convert_fusion = bf16[1024,4096]{1,0:T(8,128)(2,1)} fusion(f32[1024,4096]{1,0:T(8,128)} %fusion, bf16[256,4096]{1,0:T(8,128)(2,1)S(1)} %copy-done, f32[1024,256]{1,0:T(8,128)S(1)} %get-tuple-element.10, s32[256]{0:T(256)S(1)} %broadcast_subtract_fusion, f32[256]{0:T(256)S(1)} %get-tuple-element.7, f32[256]{0:T(256)S(1)} %pmax.7, f32[256]{0:T(256)S(1)} %copy-done.2), kind=kOutput, calls=%fused_computation | convolution fusion | flops 2157707264 | bytes 28315648 | tf_op jit(solution)/shard_map/dot_general | solution.py:55
  217.4 7.2 %convolution_convert_fusion = bf16[256,4096]{1,0:T(8,128)(2,1)} fusion(bf16[1024,4096]{1,0:T(8,128)(2,1)} %constant_dynamic-update-slice_fusion, f32[1024,256]{1,0:T(8,128)S(1)} %get-tuple-element.10, s32[256]{0:T(256)S(1)} %broadcast_subtract_fusion, f32[256]{0:T(256)S(1)} %get-tuple-element.7, f32[256]{0:T(256)S(1)} %pmax.7, f32[256]{0:T(256)S(1)} %copy-done.2), kind=kOutput, calls=%fused_computation.1 | convolution fusion | flops 2150367232 | bytes 11538432 | tf_op jit(solution)/shard_map/dot_general | solution.py:41
  225.2 56.9 %reduce-scatter.5.cloned.1.call-done = bf16[64,4096]{1,0:T(8,128)(2,1)} async-done(((bf16[1024,4096]{1,0:T(8,128)(2,1)}), bf16[64,4096]{1,0:T(8,128)(2,1)}) %reduce-scatter.5.cloned.1.call-update) | async-done | bytes 524304 | tf_op jit(solution)/shard_map/reduce_scatter | solution.py:58
  282.2 2.1 convert_element_type.20
  284.3 83.8 %reduce-scatter.3.cloned.1.call-done = bf16[256,256]{1,0:T(8,128)(2,1)} async-done(((bf16[256,4096]{1,0:T(8,128)(2,1)}), bf16[256,256]{1,0:T(8,128)(2,1)}) %reduce-scatter.3.cloned.1.call-update) | async-done | bytes 131088 | tf_op jit(solution)/shard_map/reduce_scatter | solution.py:42
  (58 shorter events, 23.9 us)
Async XLA Ops:
  7.2 118.8 %copy-start = (bf16[256,4096]{1,0:T(8,128)(2,1)S(1)}, bf16[256,4096]{1,0:T(8,128)(2,1)}, u32[]{:S(2)}) copy-start(bf16[256,4096]{1,0:T(8,128)(2,1)} %param.8) | copy-start | bytes 6291460
  7.2 28.0 %copy-start.1 = (bf16[64,4096]{1,0:T(8,128)(2,1)S(1)}, bf16[64,4096]{1,0:T(8,128)(2,1)}, u32[]{:S(2)}) copy-start(bf16[64,4096]{1,0:T(8,128)(2,1)} %param.9) | copy-start | bytes 1572868
  7.2 82.9 %all-gather.5.cloned.1.call-start = ((), (), s32[]{:S(2)}) async-start(), calls=%async_computation.4 | async-start | bytes 2228224 | tf_op jit(solution)/shard_map/all_gather | solution.py:49
  7.9 106.9 %all-gather.3.cloned.1.call-start = ((), (), s32[]{:S(2)}) async-start(), calls=%async_computation.3 | async-start | bytes 2228224 | tf_op jit(solution)/shard_map/all_gather | solution.py:47
  8.0 28.0 %collective-permute-start = (bf16[64,4096]{1,0:T(8,128)(2,1)}, bf16[64,4096]{1,0:T(8,128)(2,1)}, u32[]{:S(2)}, u32[]{:S(2)}) collective-permute-start(bf16[64,4096]{1,0:T(8,128)(2,1)} %param.9), channel_id=1, source_target_pairs={{0,16},{16,32},{32,48},{48,64},{64,80},{80,96},{96,112},{112,128},... | collective-permute-start | bytes 1572872 | tf_op jit(solution)/shard_map/ppermute | solution.py:18
  8.0 28.0 %collective-permute-start.1 = (bf16[64,4096]{1,0:T(8,128)(2,1)}, bf16[64,4096]{1,0:T(8,128)(2,1)S(1)}, u32[]{:S(2)}, u32[]{:S(2)}) collective-permute-start(bf16[64,4096]{1,0:T(8,128)(2,1)} %param.9), channel_id=1, source_target_pairs={{0,240},{16,0},{32,16},{48,32},{64,48},{80,64},{96,80},{112,96},{1... | collective-permute-start | bytes 1572872 | tf_op jit(solution)/shard_map/ppermute | solution.py:23
  9.8 272.4 %reduce-scatter.5.cloned.1.call-start = ((), (), s32[]{:S(2)}) async-start(), calls=%async_computation.5 | async-start | bytes 8912896 | tf_op jit(solution)/shard_map/reduce_scatter | solution.py:58
  36.0 8.8 %collective-permute-start.2 = (bf16[64,4096]{1,0:T(8,128)(2,1)}, bf16[64,4096]{1,0:T(8,128)(2,1)S(1)}, u32[]{:S(2)}, u32[]{:S(2)}) collective-permute-start(bf16[64,4096]{1,0:T(8,128)(2,1)} %collective-permute-done), channel_id=1, source_target_pairs={{0,16},{16,32},{32,48},{48,64},{64,80},{80,96},{96,112},{112,128},... | collective-permute-start | bytes 1572872 | tf_op jit(solution)/shard_map/ppermute | solution.py:18
  36.0 8.8 %collective-permute-start.3 = (bf16[64,4096]{1,0:T(8,128)(2,1)S(1)}, bf16[64,4096]{1,0:T(8,128)(2,1)S(1)}, u32[]{:S(2)}, u32[]{:S(2)}) collective-permute-start(bf16[64,4096]{1,0:T(8,128)(2,1)S(1)} %collective-permute-done.1), channel_id=1, source_target_pairs={{0,240},{16,0},{32,16},{48,32},{64,48},{80,64},{96,80},{112,96},{1... | collective-permute-start | bytes 1572872 | tf_op jit(solution)/shard_map/ppermute | solution.py:23
  44.8 8.6 %collective-permute-start.4 = (bf16[64,4096]{1,0:T(8,128)(2,1)S(1)}, bf16[64,4096]{1,0:T(8,128)(2,1)S(1)}, u32[]{:S(2)}, u32[]{:S(2)}) collective-permute-start(bf16[64,4096]{1,0:T(8,128)(2,1)S(1)} %collective-permute-done.2), channel_id=1, source_target_pairs={{0,16},{16,32},{32,48},{48,64},{64,80},{80,96},{96,112},{112,128},... | collective-permute-start | bytes 1572872 | tf_op jit(solution)/shard_map/ppermute | solution.py:18
  44.8 8.6 %collective-permute-start.5 = (bf16[64,4096]{1,0:T(8,128)(2,1)S(1)}, bf16[64,4096]{1,0:T(8,128)(2,1)S(1)}, u32[]{:S(2)}, u32[]{:S(2)}) collective-permute-start(bf16[64,4096]{1,0:T(8,128)(2,1)S(1)} %collective-permute-done.3), channel_id=1, source_target_pairs={{0,240},{16,0},{32,16},{48,32},{64,48},{80,64},{96,80},{112,96},{1... | collective-permute-start | bytes 1572872 | tf_op jit(solution)/shard_map/ppermute | solution.py:23
  53.4 8.6 %collective-permute-start.6 = (bf16[64,4096]{1,0:T(8,128)(2,1)S(1)}, bf16[64,4096]{1,0:T(8,128)(2,1)S(1)}, u32[]{:S(2)}, u32[]{:S(2)}) collective-permute-start(bf16[64,4096]{1,0:T(8,128)(2,1)S(1)} %collective-permute-done.4), channel_id=1, source_target_pairs={{0,16},{16,32},{32,48},{48,64},{64,80},{80,96},{96,112},{112,128},... | collective-permute-start | bytes 1572872 | tf_op jit(solution)/shard_map/ppermute | solution.py:18
  53.4 8.9 %collective-permute-start.7 = (bf16[64,4096]{1,0:T(8,128)(2,1)S(1)}, bf16[64,4096]{1,0:T(8,128)(2,1)S(1)}, u32[]{:S(2)}, u32[]{:S(2)}) collective-permute-start(bf16[64,4096]{1,0:T(8,128)(2,1)S(1)} %collective-permute-done.5), channel_id=1, source_target_pairs={{0,240},{16,0},{32,16},{48,32},{64,48},{80,64},{96,80},{112,96},{1... | collective-permute-start | bytes 1572872 | tf_op jit(solution)/shard_map/ppermute | solution.py:23
  62.0 8.6 %collective-permute-start.8 = (bf16[64,4096]{1,0:T(8,128)(2,1)S(1)}, bf16[64,4096]{1,0:T(8,128)(2,1)S(1)}, u32[]{:S(2)}, u32[]{:S(2)}) collective-permute-start(bf16[64,4096]{1,0:T(8,128)(2,1)S(1)} %collective-permute-done.6), channel_id=1, source_target_pairs={{0,16},{16,32},{32,48},{48,64},{64,80},{80,96},{96,112},{112,128},... | collective-permute-start | bytes 1572872 | tf_op jit(solution)/shard_map/ppermute | solution.py:18
  62.4 8.9 %collective-permute-start.9 = (bf16[64,4096]{1,0:T(8,128)(2,1)S(1)}, bf16[64,4096]{1,0:T(8,128)(2,1)S(1)}, u32[]{:S(2)}, u32[]{:S(2)}) collective-permute-start(bf16[64,4096]{1,0:T(8,128)(2,1)S(1)} %collective-permute-done.7), channel_id=1, source_target_pairs={{0,240},{16,0},{32,16},{48,32},{64,48},{80,64},{96,80},{112,96},{1... | collective-permute-start | bytes 1572872 | tf_op jit(solution)/shard_map/ppermute | solution.py:23
  70.7 8.6 %collective-permute-start.10 = (bf16[64,4096]{1,0:T(8,128)(2,1)S(1)}, bf16[64,4096]{1,0:T(8,128)(2,1)S(1)}, u32[]{:S(2)}, u32[]{:S(2)}) collective-permute-start(bf16[64,4096]{1,0:T(8,128)(2,1)S(1)} %collective-permute-done.8), channel_id=1, source_target_pairs={{0,16},{16,32},{32,48},{48,64},{64,80},{80,96},{96,112},{112,128},... | collective-permute-start | bytes 1572872 | tf_op jit(solution)/shard_map/ppermute | solution.py:18
  71.3 8.9 %collective-permute-start.11 = (bf16[64,4096]{1,0:T(8,128)(2,1)S(1)}, bf16[64,4096]{1,0:T(8,128)(2,1)S(1)}, u32[]{:S(2)}, u32[]{:S(2)}) collective-permute-start(bf16[64,4096]{1,0:T(8,128)(2,1)S(1)} %collective-permute-done.9), channel_id=1, source_target_pairs={{0,240},{16,0},{32,16},{48,32},{64,48},{80,64},{96,80},{112,96},{1... | collective-permute-start | bytes 1572872 | tf_op jit(solution)/shard_map/ppermute | solution.py:23
  79.3 8.8 %collective-permute-start.12 = (bf16[64,4096]{1,0:T(8,128)(2,1)S(1)}, bf16[64,4096]{1,0:T(8,128)(2,1)S(1)}, u32[]{:S(2)}, u32[]{:S(2)}) collective-permute-start(bf16[64,4096]{1,0:T(8,128)(2,1)S(1)} %collective-permute-done.10), channel_id=1, source_target_pairs={{0,16},{16,32},{32,48},{48,64},{64,80},{80,96},{96,112},{112,128},... | collective-permute-start | bytes 1572872 | tf_op jit(solution)/shard_map/ppermute | solution.py:18
  80.2 9.0 %collective-permute-start.13 = (bf16[64,4096]{1,0:T(8,128)(2,1)S(1)}, bf16[64,4096]{1,0:T(8,128)(2,1)S(1)}, u32[]{:S(2)}, u32[]{:S(2)}) collective-permute-start(bf16[64,4096]{1,0:T(8,128)(2,1)S(1)} %collective-permute-done.11), channel_id=1, source_target_pairs={{0,240},{16,0},{32,16},{48,32},{64,48},{80,64},{96,80},{112,96},{1... | collective-permute-start | bytes 1572872 | tf_op jit(solution)/shard_map/ppermute | solution.py:23
  88.1 37.1 %collective-permute-start.14 = (bf16[64,4096]{1,0:T(8,128)(2,1)S(1)}, bf16[64,4096]{1,0:T(8,128)(2,1)S(1)}, u32[]{:S(2)}, u32[]{:S(2)}) collective-permute-start(bf16[64,4096]{1,0:T(8,128)(2,1)S(1)} %collective-permute-done.12), channel_id=1, source_target_pairs={{0,16},{16,32},{32,48},{48,64},{64,80},{80,96},{96,112},{112,128},... | collective-permute-start | bytes 1572872 | tf_op jit(solution)/shard_map/ppermute | solution.py:18
  126.0 79.7 %copy-start.2 = (f32[256]{0:T(256)S(1)}, f32[256]{0:T(256)}, u32[]{:S(2)}) copy-start(f32[256]{0:T(256)} %param.11) | copy-start | bytes 3076
  217.2 150.9 %reduce-scatter.3.cloned.1.call-start = ((), (), s32[]{:S(2)}) async-start(), calls=%async_computation.2 | async-start | bytes 2228224 | tf_op jit(solution)/shard_map/reduce_scatter | solution.py:42
Sparse Core Ops, SparseCore 0:
  10.5 52.5 all-gather.4
  65.5 49.3 all-gather.2
  217.3 64.8 reduce-scatter.4
  286.2 81.8 reduce-scatter.2
